TPU v7x, 256 devices: a whole 4x4x8 slice. The times are simulated.
256 devices in a mesh: cfg: 2 (over core), tok: 8 (over z), mlp: 16 (over x, y).
Axes of the slice: x: 4, y: 4, z: 8, core: 2. Of those that a mesh axis runs over, the one named last changes fastest.
Arguments:
- hidden: bfloat16 [2, 1536, 4, 3072], P('cfg', ('tok', 'mlp')), may hold values from -6 to 6
- latents: float32 [1536, 4, 64], P(('tok', 'mlp'), None, 'cfg'), may hold values from -6 to 6
- vec: float32 [2, 4, 3072], P('cfg'), may hold values from -9 to 9
- slot_token: int32 [4, 1536], replicated, may hold values from 0 to 1535, each once within a row
- text_len: int32 [2, 4], P('cfg'), may hold values from 64 to 512, as said below
- step_index: int32 [1], replicated, may hold values from 0 to 27
- guidance: float32 [1], replicated, may hold values from 2 to 5
- w_mod: bfloat16 [3072, 15360], P(None, ('tok', 'mlp')), may hold values from -0.109375 to 0.109375
- w_qkv: bfloat16 [1, 3072, 3, 2048], P(None, 'cfg', None, 'mlp'), may hold values from -0.109375 to 0.109375
- w_mlp_in: bfloat16 [1, 3072, 12288], P(None, 'cfg', 'mlp'), may hold values from -0.109375 to 0.109375
- qk_gain: float32 [1, 2, 128], replicated, may hold values from 1.5 to 2.5
- w_attn_out: bfloat16 [1, 2048, 3072], P(None, 'mlp', 'cfg'), may hold values from -0.125 to 0.125
- w_mlp_out: bfloat16 [1, 12288, 3072], P(None, 'mlp', 'cfg'), may hold values from -0.0546875 to 0.0546875
- w_final: bfloat16 [3072, 64], replicated, may hold values from -0.109375 to 0.109375
Outputs:
- velocity: float32 [1536, 4, 64], P(('tok', 'mlp'), None, 'cfg')
- latents_next: float32 [1536, 4, 64], P(('tok', 'mlp'), None, 'cfg')
- stream_out: bfloat16 [2, 1536, 4, 3072], P('cfg', ('tok', 'mlp'))
Inputs may be any that keep to these rules, and one draw needn't show every extreme that they name: `text_len`: real text tokens of each request; its other text slots are padding; exactly one request has all 512. `slot_token`: row p lists the token held by each slot of request p: text tokens are 0 to 511, image tokens follow row by row on the 32 x 32 grid.
All inputs are finite; a program needn't handle non-finite values.
Results may differ from a plain program's by a relative error of at most 0.018.
Values may be sent and summed in bfloat16 or wider, within the bound.
A program may use at most 128 MiB of HBM per device.

v0:
```python
import math
import jax
import jax.numpy as jnp
from jax import lax
from jax.sharding import PartitionSpec as P

LAYERS = 1
SIDE = 32
TXT = 512
STEPS = 28
EPSILON = 1e-06
ROPE_BASE = 10000.0
TIME_SHIFT = 3.0


def swapped(value, axis, apart):
    return lax.ppermute(value, axis, [(i, i ^ 1 << apart) for i in range(lax.axis_size(axis))])


def layer_norm(values):
    average = jnp.mean(values, axis=-1, keepdims=True)
    centred = values - average
    spread = jnp.mean(centred * centred, axis=-1, keepdims=True)
    return centred * lax.rsqrt(spread + EPSILON)


def rms_norm(values, gains):
    return values * lax.rsqrt(jnp.mean(values * values, axis=-1, keepdims=True) + EPSILON) * gains


def rope_table(tokens, head_size, text_count, side_count):
    pair_count = head_size // 2
    first_pairs = head_size // 16
    axis_pairs = (head_size - head_size // 8) // 4
    pair_index = jnp.arange(pair_count).astype(jnp.float32)
    in_rows = (pair_index >= first_pairs) & (pair_index < first_pairs + axis_pairs)
    in_cols = pair_index >= first_pairs + axis_pairs
    log_base = math.log(ROPE_BASE)
    freq_rows = jnp.where(
        in_rows, jnp.exp(-log_base * (pair_index - first_pairs) / axis_pairs), 0.0
    )
    freq_cols = jnp.where(
        in_cols, jnp.exp(-log_base * (pair_index - first_pairs - axis_pairs) / axis_pairs), 0.0
    )
    is_image = tokens >= text_count
    image_pos = jnp.where(is_image, tokens - text_count, 0)
    row_pos = (image_pos // side_count).astype(jnp.float32)
    col_pos = (image_pos % side_count).astype(jnp.float32)
    angles = row_pos[..., None] * freq_rows + col_pos[..., None] * freq_cols
    return (jnp.cos(angles), jnp.sin(angles))


def apply_rope(values, cosine, sine_table):
    even_part = values[..., 0::2]
    odd_part = values[..., 1::2]
    return jnp.concatenate(
        [even_part * cosine - odd_part * sine_table, even_part * sine_table + odd_part * cosine],
        axis=-1,
    )


def sigma_at(position, steps_total):
    remain = 1.0 - position / steps_total
    return TIME_SHIFT * remain / (1.0 + (TIME_SHIFT - 1.0) * remain)


def on_device(
    hidden,
    latents,
    vec,
    slot_token,
    text_len,
    step_index,
    guidance,
    w_mod,
    w_qkv,
    w_mlp_in,
    qk_gain,
    w_attn_out,
    w_mlp_out,
    w_final,
):
    rows_dev = hidden.shape[1]
    prompts = hidden.shape[2]
    model_width = hidden.shape[3]
    head_size = qk_gain.shape[-1]
    mlp_count = lax.axis_size("mlp")
    tile_rows = rows_dev * mlp_count
    tok_index = lax.axis_index("tok")
    mlp_index = lax.axis_index("mlp")
    half_index = lax.axis_index("cfg")
    first_half = half_index == 0
    stream = hidden[0]
    silu_vec = jax.nn.silu(vec[0]).astype(jnp.bfloat16)
    mod_part = jnp.dot(silu_vec, w_mod, preferred_element_type=jnp.float32)
    modulation = lax.all_gather(mod_part, ("tok", "mlp"), axis=1, tiled=True)
    key_valid = ((slot_token >= TXT) | (slot_token < text_len[0][:, None])).astype(jnp.float32)
    tile_tokens = lax.dynamic_slice_in_dim(slot_token, tok_index * tile_rows, tile_rows, 1).T
    cosine, sine_table = rope_table(tile_tokens, head_size, TXT, SIDE)
    shift_mod = modulation[:, 0:model_width]
    scale_mod = modulation[:, model_width : 2 * model_width]
    gate_mod = modulation[:, 2 * model_width : 3 * model_width]
    normed = (
        layer_norm(stream.astype(jnp.float32)) * (1.0 + scale_mod[None]) + shift_mod[None]
    ).astype(jnp.bfloat16)
    tile_input = lax.all_gather(normed, "mlp", axis=0, tiled=True)
    qkv_weight = w_qkv[0]
    unit_weight = w_mlp_in[0]
    qkv_cols = qkv_weight.shape[1] * qkv_weight.shape[2]
    pieces = (
        lax.all_gather(qkv_weight, "cfg", axis=0, tiled=True),
        lax.all_gather(unit_weight, "cfg", axis=0, tiled=True),
    )
    number = pieces[0].shape[0]
    qkv_piece = pieces[0].reshape(number, qkv_cols)
    qkv_pre = jnp.einsum("tpd,dk->tpk", tile_input, qkv_piece, preferred_element_type=jnp.float32)
    unit_pre = jnp.einsum("tpd,dk->tpk", tile_input, pieces[1], preferred_element_type=jnp.float32)
    heads_dev = qkv_weight.shape[2] // head_size
    projected = qkv_pre.reshape(tile_rows, prompts, 3, heads_dev, head_size)
    queries = apply_rope(
        rms_norm(projected[:, :, 0], qk_gain[0, 0]), cosine[:, :, None], sine_table[:, :, None]
    ).astype(jnp.bfloat16)
    keys_rot = apply_rope(
        rms_norm(projected[:, :, 1], qk_gain[0, 1]), cosine[:, :, None], sine_table[:, :, None]
    ).astype(jnp.bfloat16)
    values = projected[:, :, 2].astype(jnp.bfloat16)
    activation = jax.nn.gelu(unit_pre, approximate=True).astype(jnp.bfloat16)
    keys_piece = lax.all_gather(keys_rot, "tok", axis=0, tiled=True)
    values_piece = lax.all_gather(values, "tok", axis=0, tiled=True)
    scores = jnp.einsum(
        "sphe,tphe->phst", queries, keys_piece, preferred_element_type=jnp.float32
    ) / math.sqrt(head_size)
    softened = jnp.exp(scores) * key_valid[:, None, None, :]
    numerator = jnp.einsum(
        "phst,tphe->sphe",
        softened.astype(jnp.bfloat16),
        values_piece,
        preferred_element_type=jnp.float32,
    )
    numerator, denominator = (numerator, jnp.sum(softened, axis=-1))
    attended = (numerator / jnp.transpose(denominator, (2, 0, 1))[..., None]).astype(jnp.bfloat16)
    attended = attended.reshape(tile_rows, prompts, heads_dev * head_size)
    out_attn = lax.all_gather(w_attn_out[0], "cfg", axis=1, tiled=True)
    out_units = lax.all_gather(w_mlp_out[0], "cfg", axis=1, tiled=True)
    branch_out = lax.psum_scatter(
        (
            jnp.einsum("tpk,kd->tpd", attended, out_attn, preferred_element_type=jnp.float32)
            + jnp.einsum("tpk,kd->tpd", activation, out_units, preferred_element_type=jnp.float32)
        ).astype(jnp.bfloat16),
        "mlp",
        scatter_dimension=0,
        tiled=True,
    ).astype(jnp.float32)
    stream = (stream.astype(jnp.float32) + gate_mod[None] * branch_out).astype(jnp.bfloat16)
    final_lo = 3 * LAYERS * model_width
    final_shift = modulation[:, final_lo : final_lo + model_width]
    final_scale = modulation[:, final_lo + model_width : final_lo + 2 * model_width]
    final_normed = (
        layer_norm(stream.astype(jnp.float32)) * (1.0 + final_scale[None]) + final_shift[None]
    ).astype(jnp.bfloat16)
    own_first = (tok_index * mlp_count + mlp_index) * rows_dev
    own_tokens = lax.dynamic_slice_in_dim(slot_token, own_first, rows_dev, 1).T
    half_velocity = jnp.einsum(
        "rpd,dc->rpc", final_normed, w_final, preferred_element_type=jnp.float32
    )
    half_velocity = jnp.where((own_tokens >= TXT)[:, :, None], half_velocity, 0.0)
    channel_half = latents.shape[2]
    own_part = lax.dynamic_slice_in_dim(half_velocity, half_index * channel_half, channel_half, 2)
    sent_part = lax.dynamic_slice_in_dim(
        half_velocity, (1 - half_index) * channel_half, channel_half, 2
    )
    partner = swapped(sent_part, "cfg", 0)
    cond_part = jnp.where(first_half, own_part, partner)
    uncond_part = jnp.where(first_half, partner, own_part)
    velocity = uncond_part + guidance[0] * (cond_part - uncond_part)
    current = step_index[0].astype(jnp.float32)
    step_size = sigma_at(current + 1.0, STEPS) - sigma_at(current, STEPS)
    return (velocity, latents + step_size * velocity, stream[None])


def solution(mesh):
    return jax.shard_map(
        on_device,
        mesh=mesh,
        in_specs=(
            P("cfg", ("tok", "mlp"), None, None),
            P(("tok", "mlp"), None, "cfg"),
            P("cfg", None, None),
            P(),
            P("cfg", None),
            P(),
            P(),
            P(None, ("tok", "mlp")),
            P(None, "cfg", None, "mlp"),
            P(None, "cfg", "mlp"),
            P(),
            P(None, "mlp", "cfg"),
            P(None, "mlp", "cfg"),
            P(),
        ),
        out_specs=(
            P(("tok", "mlp"), None, "cfg"),
            P(("tok", "mlp"), None, "cfg"),
            P("cfg", ("tok", "mlp"), None, None),
        ),
        check_vma=False,
    )
```

profile of v0, /device:TPU:1, one launch (start us, length us, event | category | flops | bytes accessed | tf_op | source)
XLA Modules:
  0.0 687.4 jit_solution(511680488462771938)
XLA Ops:
  7.2 2.5 copy.32
  10.2 295.8 %all-gather.5 = f32[128,120,4]{1,2,0:T(4,128)S(1)} all-gather(f32[1,120,4]{1,2,0:T(4,128)S(1)} %convolution_bitcast_fusion), channel_id=1, replica_groups=mesh['cfg'=2,'tok'=8,'mlp'=16] {'tok','mlp'}, dimensions={0}, use_global_device_ids=true | all-gather | bytes 247680 | tf_op jit(solution)/shard_map/all_gather | solution.py:96
  306.8 1.0 fusion.67
  307.9 0.7 all-gather.21.cloned.1.call-update
  308.7 0.5 all-gather.23.cloned.1.call-update
  309.3 0.5 compare_select_fusion
  309.8 0.8 fusion.84
  310.6 103.2 %all-gather.13.cloned.1.call-done = bf16[192,4,3072]{2,1,0:T(4,128)(2,1)} async-done(((bf16[12,4,3072]{2,1,0:T(4,128)(2,1)}), bf16[192,4,3072]{2,1,0:T(4,128)(2,1)}) %all-gather.13.cloned.1.call-update) | async-done | bytes 4718608 | tf_op jit(solution)/shard_map/all_gather | solution.py:106
  413.8 5.2 fusion.24
  419.1 0.4 multiply_reduce_fusion.1
  419.7 6.6 slice.49
  426.4 7.3 %slice.50 = f32[192,4,1,64]{3,0,1,2:T(8,128)} slice(f32[192,4,1,128]{3,0,1,2:T(8,128)S(1)} %get-tuple-element.18), slice={[0:192:1], [0:4:1], [0:1:1], [1:128:2]} | slice | bytes 393216 | tf_op jit(solution)/shard_map/slice | solution.py:55
  433.7 6.6 slice.53
  440.3 7.5 %slice.54 = f32[192,4,1,64]{3,0,1,2:T(8,128)} slice(f32[192,4,1,128]{3,0,1,2:T(8,128)S(1)} %get-tuple-element.19), slice={[0:192:1], [0:4:1], [0:1:1], [1:128:2]} | slice | bytes 393216 | tf_op jit(solution)/shard_map/slice | solution.py:55
  447.9 4.1 fusion.77
  451.9 0.8 pad_maximum_fusion
  452.8 0.7 slice.80
  453.6 3.4 all-gather.2
  457.1 10.6 %fusion.14 = bf16[192,4,768]{2,0,1:T(8,128)(2,1)} fusion(bf16[1,3072,768]{2,1,0:T(8,128)(2,1)} %all-gather.21.cloned.1.call-done, bf16[192,4,3072]{2,1,0:T(4,128)(2,1)} %all-gather.13.cloned.1.call-done), kind=kOutput, calls=%fused_computation.17 | convolution fusion | flops 3629187072 | bytes 10616832 | tf_op jit(solution)/shard_map/tpd,dk->tpk/dot_general | solution.py:117
  467.7 10.2 %fusion = f32[192,4,3072]{2,0,1:T(8,128)} fusion(bf16[192,4,768]{2,0,1:T(8,128)(2,1)} %fusion.14, bf16[1,768,3072]{2,1,0:T(8,128)(2,1)} %all-gather.23.cloned.1.call-done), kind=kOutput, calls=%fused_computation.1 | convolution fusion | flops 3623878656 | bytes 15335424 | tf_op jit(solution)/shard_map/tpk,kd->tpd/dot_general | solution.py:148
  477.9 19.1 %all-gather.15.cloned.1.call-done = bf16[1536,4,1,128]{3,0,1,2:T(8,128)(2,1)} async-done(((bf16[192,4,1,128]{3,0,1,2:T(8,128)(2,1)}), bf16[1536,4,1,128]{3,0,1,2:T(8,128)(2,1)}) %all-gather.15.cloned.1.call-update) | async-done | bytes 1572880 | tf_op jit(solution)/shard_map/all_gather | solution.py:128
  497.0 4.0 fusion.92
  501.1 36.8 %all-gather.19.cloned.1.call-done = bf16[1536,4,1,1,128]{4,0,2,1,3:T(8,128)(2,1)} async-done(((bf16[192,4,1,1,128]{4,0,2,1,3:T(8,128)(2,1)}), bf16[1536,4,1,1,128]{4,0,2,1,3:T(8,128)(2,1)}) %all-gather.19.cloned.1.call-update) | async-done | bytes 1572880 | tf_op jit(solution)/shard_map/all_gather | solution.py:129
  537.9 7.8 %add_convert_fusion = bf16[192,4,3072]{2,0,1:T(8,128)(2,1)} fusion(f32[192,4,3072]{2,0,1:T(8,128)} %fusion, bf16[1536,4,1,1,128]{4,0,2,1,3:T(8,128)(2,1)} %all-gather.19.cloned.1.call-done, bf16[4,192,1536]{2,1,0:T(8,128)(2,1)} %get-tuple-element.36, bf16[1,128,3072]{2,1,0:T(8,128)(2,1)S(1)} %all-gather.2, f32[192,4]{0,1:T(4,128)S(1)} %bitcast.167), kind=kOutput, calls=%fused_computation | convolution fusion | flops 910884864 | bytes 18877440 | tf_op jit(solution)/shard_map/tpk,kd->tpd/dot_general | solution.py:147
  545.7 8.1 %copy.36 = bf16[192,4,3072]{2,1,0:T(4,128)(2,1)} copy(bf16[192,4,3072]{2,0,1:T(8,128)(2,1)} %add_convert_fusion) | data formatting | bytes 9437184 | tf_op jit(solution)/shard_map/convert_element_type | solution.py:149
  553.9 0.6 copy-done.11
  554.5 0.6 dynamic-slice
  555.8 119.0 %all-reduce.3.cloned.1.call-done = bf16[192,4,3072]{2,1,0:T(4,128)(2,1)} async-done(((bf16[192,4,3072]{2,1,0:T(4,128)(2,1)}), bf16[192,4,3072]{2,1,0:T(4,128)(2,1)}) %all-reduce.3.cloned.1.call-update) | async-done | bytes 4718608
  674.8 1.3 convert_reduce_fusion
  677.1 0.7 collective-permute-start
  679.3 0.6 copy.39
  679.9 0.6 copy.40
  (59 shorter events, 3.2 us)
Async XLA Ops:
  7.2 2.7 copy-start
  7.2 2.7 copy-start.10
  7.2 299.1 %copy-start.1 = (bf16[1,12,4,3072]{3,2,1,0:T(4,128)(2,1)S(1)}, bf16[1,12,4,3072]{3,2,1,0:T(4,128)(2,1)}, u32[]{:S(2)}) copy-start(bf16[1,12,4,3072]{3,2,1,0:T(4,128)(2,1)} %param.14) | copy-start | bytes 884740
  7.2 303.4 %all-gather.17.cloned.1.call-start = ((), (), s32[]{:S(2)}) async-start(), calls=%async_computation.2 | async-start | bytes 3538944 | tf_op jit(solution)/shard_map/all_gather | solution.py:111
  9.8 404.0 %all-gather.13.cloned.1.call-start = ((), (), s32[]{:S(2)}) async-start(), calls=%async_computation | async-start | bytes 5013504 | tf_op jit(solution)/shard_map/all_gather | solution.py:106
  307.9 2.7 copy-start.7
  307.9 149.2 %all-gather.21.cloned.1.call-start = ((), (), s32[]{:S(2)}) async-start(), calls=%async_computation.4 | async-start | bytes 7077888 | tf_op jit(solution)/shard_map/all_gather | solution.py:112
  308.6 159.0 %all-gather.23.cloned.1.call-start = ((), (), s32[]{:S(2)}) async-start(), calls=%async_computation.5 | async-start | bytes 7077888 | tf_op jit(solution)/shard_map/all_gather | solution.py:144
  309.2 187.8 %all-gather.15.cloned.1.call-start = ((), (), s32[]{:S(2)}) async-start(), calls=%async_computation.1 | async-start | bytes 1769472 | tf_op jit(solution)/shard_map/all_gather | solution.py:128
  447.9 9.2 %copy-start.8 = (s32[1,4]{1,0:T(1,128)S(1)}, s32[1,4]{1,0:T(1,128)}, u32[]{:S(2)}) copy-start(s32[1,4]{1,0:T(1,128)} %param.18) | copy-start | bytes 52
  451.9 5.1 copy-start.5
  452.7 85.2 %all-gather.19.cloned.1.call-start = ((), (), s32[]{:S(2)}) async-start(), calls=%async_computation.3 | async-start | bytes 1769472 | tf_op jit(solution)/shard_map/all_gather | solution.py:129
  453.5 221.3 %all-reduce.3.cloned.1.call-start = ((), (), s32[]{:S(2)}) async-start(), calls=%async_computation.6 | async-start | bytes 9437184
  467.7 29.4 %copy-start.3 = (bf16[192,4,64]{2,0,1:T(8,128)(2,1)S(1)}, bf16[192,4,64]{2,0,1:T(8,128)(2,1)}, u32[]{:S(2)}) copy-start(bf16[192,4,64]{2,0,1:T(8,128)(2,1)} %get-tuple-element.20) | copy-start | bytes 294916
  467.7 29.4 %copy-start.4 = (bf16[192,4,64]{2,0,1:T(8,128)(2,1)S(1)}, bf16[192,4,64]{2,0,1:T(8,128)(2,1)}, u32[]{:S(2)}) copy-start(bf16[192,4,64]{2,0,1:T(8,128)(2,1)} %get-tuple-element.21) | copy-start | bytes 294916
  553.8 0.7 copy-start.11
  553.8 122.9 %copy-start.9 = (bf16[3072,64]{0,1:T(8,128)(2,1)S(1)}, bf16[3072,64]{0,1:T(8,128)(2,1)}, u32[]{:S(2)}) copy-start(bf16[3072,64]{0,1:T(8,128)(2,1)} %param.27) | copy-start | bytes 1179652
  553.8 125.4 %copy-start.6 = (f32[12,4,32]{2,1,0:T(4,128)S(1)}, f32[12,4,32]{2,1,0:T(4,128)}, u32[]{:S(2)}) copy-start(f32[12,4,32]{2,1,0:T(4,128)} %param.15) | copy-start | bytes 18436
  676.1 4.5 copy-start.2
  677.1 2.1 collective-permute-start
Sparse Core Ops, SparseCore 0:
  9.9 20.8 all-gather.16
  308.0 105.7 all-gather.12
  415.6 20.2 all-gather.20
  437.5 21.6 all-gather.22
  460.8 36.1 all-gather.14
  499.3 38.5 all-gather.18
  554.0 120.7 all-reduce.2
where the time goes:
time: 688 us; the launch traced here: 687 us
  blocking collectives  299 us (43%)
  waiting for transfers between devices  279 us (41%)
  local copies, waits for them, and re-layouts  42.4 us (6%)
  matrix products  38.4 us (6%)
  between operations  16.4 us (2%)
  other arithmetic  10.6 us (2%)
    all_gather x1, blocking collectives, on_device(): modulation = lax.all_gather(mod_part, ('tok', 'mlp'), axis=1, tiled=True)  296 us
    unnamed x8, waiting for transfers between devices  120 us
    all_gather x1, waiting for transfers between devices, on_device(): tile_input = lax.all_gather(normed, 'mlp', axis=0, tiled=True)  103 us
    all_gather x1, waiting for transfers between devices, on_device(): values_piece = lax.all_gather(values, 'tok', axis=0, tiled=True)  36.8 us
    all_gather x1, waiting for transfers between devices, on_device(): keys_piece = lax.all_gather(keys_rot, 'tok', axis=0, tiled=True)  19.1 us
    slice x2, local copies, waits for them, and re-layouts, apply_rope(): odd_part = values[..., 1::2]  14.9 us
  transfers between devices with their start and end apart: 8, of which 4 were waited for; matrix products, arithmetic and copies ran while one was open for 10% of the time, Pallas kernels for 0%

commit v1 on v0

--- a/solution.py
+++ b/solution.py
@@ -125,8 +125,11 @@
     ).astype(jnp.bfloat16)
     values = projected[:, :, 2].astype(jnp.bfloat16)
     activation = jax.nn.gelu(unit_pre, approximate=True).astype(jnp.bfloat16)
-    keys_piece = lax.all_gather(keys_rot, "tok", axis=0, tiled=True)
-    values_piece = lax.all_gather(values, "tok", axis=0, tiled=True)
+    keys_piece, values_piece = jnp.split(
+        lax.all_gather(jnp.concatenate([keys_rot, values], axis=1), "tok", axis=0, tiled=True),
+        [keys_rot.shape[1]],
+        axis=1,
+    )
     scores = jnp.einsum(
         "sphe,tphe->phst", queries, keys_piece, preferred_element_type=jnp.float32
     ) / math.sqrt(head_size)

time: 688 us -> 656 us (0.953)
  waiting for transfers between devices: 279 us -> 248 us
    all_gather x2 -> x1, waiting for transfers between devices: 55.9 us -> 28.4 us  [on_device(): lax.all_gather(jnp.concatenate([keys_rot, values], axis=1), 'tok', axis=0...]
    unnamed x8 -> x7, waiting for transfers between devices: 120 us -> 117 us
  transfers between devices with their start and end apart: 8 -> 7, of which waited for: 4 -> 3; matrix products, arithmetic and copies ran while one was open for 10% -> 10% of each run, Pallas kernels for 0% -> 0%
where the time goes in v1:
time: 656 us
  blocking collectives  299 us (46%)
  waiting for transfers between devices  248 us (38%)
  local copies, waits for them, and re-layouts  41.7 us (6%)
  matrix products  38.5 us (6%)
  between operations  16.4 us (2%)
  other arithmetic  10.8 us (2%)
    all_gather x1, blocking collectives, on_device(): modulation = lax.all_gather(mod_part, ('tok', 'mlp'), axis=1, tiled=True)  296 us
    unnamed x7, waiting for transfers between devices  117 us
    all_gather x1, waiting for transfers between devices, on_device(): tile_input = lax.all_gather(normed, 'mlp', axis=0, tiled=True)  103 us
    all_gather x1, waiting for transfers between devices, on_device(): lax.all_gather(jnp.concatenate([keys_rot, values], axis=1), 'tok', axis=0...  28.4 us
    slice x2, local copies, waits for them, and re-layouts, apply_rope(): even_part = values[..., 0::2]  14.7 us
    slice x2, local copies, waits for them, and re-layouts, apply_rope(): odd_part = values[..., 1::2]  13.4 us
  transfers between devices with their start and end apart: 7, of which 3 were waited for; matrix products, arithmetic and copies ran while one was open for 10% of the time, Pallas kernels for 0%

profile of v1, /device:TPU:1, one launch (start us, length us, event | category | flops | bytes accessed | tf_op | source)
XLA Modules:
  0.0 655.6 jit_solution(8687076607529613313)
XLA Ops:
  7.2 2.5 copy.34
  10.1 295.8 %all-gather.4 = f32[128,120,4]{1,2,0:T(4,128)S(1)} all-gather(f32[1,120,4]{1,2,0:T(4,128)S(1)} %convolution_bitcast_fusion), channel_id=1, replica_groups=mesh['cfg'=2,'tok'=8,'mlp'=16] {'tok','mlp'}, dimensions={0}, use_global_device_ids=true | all-gather | bytes 247680 | tf_op jit(solution)/shard_map/all_gather | solution.py:96
  305.9 0.3 reshape.289
  306.4 0.3 fusion.52
  306.8 1.0 fusion.55
  307.9 0.7 all-gather.17.cloned.1.call-update
  308.6 0.5 all-gather.19.cloned.1.call-update
  309.2 0.5 compare_select_fusion
  309.7 0.8 fusion.73
  310.6 103.2 %all-gather.11.cloned.1.call-done = bf16[192,4,3072]{2,1,0:T(4,128)(2,1)} async-done(((bf16[12,4,3072]{2,1,0:T(4,128)(2,1)}), bf16[192,4,3072]{2,1,0:T(4,128)(2,1)}) %all-gather.11.cloned.1.call-update) | async-done | bytes 4718608 | tf_op jit(solution)/shard_map/all_gather | solution.py:106
  413.8 5.2 fusion.22
  419.8 6.7 %slice.54 = f32[192,4,1,64]{3,0,1,2:T(8,128)S(1)} slice(f32[192,4,1,128]{3,0,1,2:T(8,128)S(1)} %get-tuple-element.33), slice={[0:192:1], [0:4:1], [0:1:1], [1:128:2]} | slice | bytes 393216 | tf_op jit(solution)/shard_map/slice | solution.py:55
  426.5 7.3 %slice.53 = f32[192,4,1,64]{3,0,1,2:T(8,128)} slice(f32[192,4,1,128]{3,0,1,2:T(8,128)S(1)} %get-tuple-element.33), slice={[0:192:1], [0:4:1], [0:1:1], [0:128:2]} | slice | bytes 393216 | tf_op jit(solution)/shard_map/slice | solution.py:54
  433.7 6.7 %slice.49 = f32[192,4,1,64]{3,0,1,2:T(8,128)S(1)} slice(f32[192,4,1,128]{3,0,1,2:T(8,128)S(1)} %get-tuple-element.34), slice={[0:192:1], [0:4:1], [0:1:1], [1:128:2]} | slice | bytes 393216 | tf_op jit(solution)/shard_map/slice | solution.py:55
  440.5 7.5 %slice.48 = f32[192,4,1,64]{3,0,1,2:T(8,128)} slice(f32[192,4,1,128]{3,0,1,2:T(8,128)S(1)} %get-tuple-element.34), slice={[0:192:1], [0:4:1], [0:1:1], [0:128:2]} | slice | bytes 393216 | tf_op jit(solution)/shard_map/slice | solution.py:54
  448.0 4.1 fusion.66
  452.1 0.9 pad_maximum_fusion
  453.0 3.2 all-gather.1
  456.4 10.6 %fusion.14 = bf16[192,4,768]{2,0,1:T(8,128)(2,1)} fusion(bf16[1,3072,768]{2,1,0:T(8,128)(2,1)} %all-gather.17.cloned.1.call-done, bf16[192,4,3072]{2,1,0:T(4,128)(2,1)} %all-gather.11.cloned.1.call-done), kind=kOutput, calls=%fused_computation.17 | convolution fusion | flops 3629187072 | bytes 10616832 | tf_op jit(solution)/shard_map/tpd,dk->tpk/dot_general | solution.py:117
  467.0 10.2 %fusion = f32[192,4,3072]{2,0,1:T(8,128)} fusion(bf16[192,4,768]{2,0,1:T(8,128)(2,1)} %fusion.14, bf16[1,768,3072]{2,1,0:T(8,128)(2,1)} %all-gather.19.cloned.1.call-done), kind=kOutput, calls=%fused_computation.1 | convolution fusion | flops 3623878656 | bytes 15335424 | tf_op jit(solution)/shard_map/tpk,kd->tpd/dot_general | solution.py:151
  477.2 28.4 %all-gather.13.cloned.1.call-done = bf16[1536,8,1,128]{3,0,1,2:T(8,128)(2,1)} async-done(((bf16[192,8,1,128]{3,0,1,2:T(8,128)(2,1)}), bf16[1536,8,1,128]{3,0,1,2:T(8,128)(2,1)}) %all-gather.13.cloned.1.call-update) | async-done | bytes 3145744 | tf_op jit(solution)/shard_map/all_gather | solution.py:129
  505.6 4.1 fusion.81
  509.7 7.8 %add_convert_fusion = bf16[192,4,3072]{2,0,1:T(8,128)(2,1)} fusion(f32[192,4,3072]{2,0,1:T(8,128)} %fusion, bf16[1536,8,1,128]{3,0,1,2:T(8,128)(2,1)} %all-gather.13.cloned.1.call-done, bf16[4,192,1536]{2,1,0:T(8,128)(2,1)} %get-tuple-element.32, bf16[1,128,3072]{2,1,0:T(8,128)(2,1)S(1)} %all-gather.1, f32[192,4]{0,1:T(4,128)S(1)} %bitcast.167), kind=kOutput, calls=%fused_computation | convolution fusion | flops 910884864 | bytes 18877440 | tf_op jit(solution)/shard_map/tpk,kd->tpd/dot_general | solution.py:150
  517.5 8.1 %copy.39 = bf16[192,4,3072]{2,1,0:T(4,128)(2,1)} copy(bf16[192,4,3072]{2,0,1:T(8,128)(2,1)} %add_convert_fusion) | data formatting | bytes 9437184 | tf_op jit(solution)/shard_map/convert_element_type | solution.py:152
  525.6 0.6 copy-done.12
  526.2 0.6 dynamic-slice
  527.6 115.4 %all-reduce.3.cloned.1.call-done = bf16[192,4,3072]{2,1,0:T(4,128)(2,1)} async-done(((bf16[192,4,3072]{2,1,0:T(4,128)(2,1)}), bf16[192,4,3072]{2,1,0:T(4,128)(2,1)}) %all-reduce.3.cloned.1.call-update) | async-done | bytes 4718608
  643.0 1.3 convert_reduce_fusion
  644.3 0.3 fusion.48
  645.3 0.7 collective-permute-start
  647.5 0.6 copy.42
  648.1 0.6 copy.43
  (60 shorter events, 2.6 us)
Async XLA Ops:
  7.2 2.6 copy-start
  7.2 2.6 copy-start.11
  7.2 299.0 %copy-start.1 = (bf16[1,12,4,3072]{3,2,1,0:T(4,128)(2,1)S(1)}, bf16[1,12,4,3072]{3,2,1,0:T(4,128)(2,1)}, u32[]{:S(2)}) copy-start(bf16[1,12,4,3072]{3,2,1,0:T(4,128)(2,1)} %param.14) | copy-start | bytes 884740
  7.2 303.4 %all-gather.15.cloned.1.call-start = ((), (), s32[]{:S(2)}) async-start(), calls=%async_computation.2 | async-start | bytes 3538944 | tf_op jit(solution)/shard_map/all_gather | solution.py:111
  9.8 404.0 %all-gather.11.cloned.1.call-start = ((), (), s32[]{:S(2)}) async-start(), calls=%async_computation | async-start | bytes 5013504 | tf_op jit(solution)/shard_map/all_gather | solution.py:106
  307.8 2.7 copy-start.8
  307.9 148.5 %all-gather.17.cloned.1.call-start = ((), (), s32[]{:S(2)}) async-start(), calls=%async_computation.3 | async-start | bytes 7077888 | tf_op jit(solution)/shard_map/all_gather | solution.py:112
  308.6 158.4 %all-gather.19.cloned.1.call-start = ((), (), s32[]{:S(2)}) async-start(), calls=%async_computation.4 | async-start | bytes 7077888 | tf_op jit(solution)/shard_map/all_gather | solution.py:147
  309.2 196.4 %all-gather.13.cloned.1.call-start = ((), (), s32[]{:S(2)}) async-start(), calls=%async_computation.1 | async-start | bytes 3538944 | tf_op jit(solution)/shard_map/all_gather | solution.py:129
  448.0 5.1 copy-start.3
  448.0 8.3 %copy-start.9 = (s32[1,4]{1,0:T(1,128)S(1)}, s32[1,4]{1,0:T(1,128)}, u32[]{:S(2)}) copy-start(s32[1,4]{1,0:T(1,128)} %param.18) | copy-start | bytes 52
  452.1 4.2 copy-start.6
  453.0 190.0 %all-reduce.3.cloned.1.call-start = ((), (), s32[]{:S(2)}) async-start(), calls=%async_computation.5 | async-start | bytes 9437184
  467.0 38.6 %copy-start.4 = (bf16[192,4,64]{2,0,1:T(8,128)(2,1)S(1)}, bf16[192,4,64]{2,0,1:T(8,128)(2,1)}, u32[]{:S(2)}) copy-start(bf16[192,4,64]{2,0,1:T(8,128)(2,1)} %get-tuple-element.16) | copy-start | bytes 294916
  467.0 38.6 %copy-start.5 = (bf16[192,4,64]{2,0,1:T(8,128)(2,1)S(1)}, bf16[192,4,64]{2,0,1:T(8,128)(2,1)}, u32[]{:S(2)}) copy-start(bf16[192,4,64]{2,0,1:T(8,128)(2,1)} %get-tuple-element.17) | copy-start | bytes 294916
  525.6 0.7 copy-start.12
  525.6 119.4 %copy-start.10 = (bf16[3072,64]{0,1:T(8,128)(2,1)S(1)}, bf16[3072,64]{0,1:T(8,128)(2,1)}, u32[]{:S(2)}) copy-start(bf16[3072,64]{0,1:T(8,128)(2,1)} %param.27) | copy-start | bytes 1179652
  525.6 121.8 %copy-start.7 = (f32[12,4,32]{2,1,0:T(4,128)S(1)}, f32[12,4,32]{2,1,0:T(4,128)}, u32[]{:S(2)}) copy-start(f32[12,4,32]{2,1,0:T(4,128)} %param.15) | copy-start | bytes 18436
  644.3 4.5 copy-start.2
  645.3 2.1 collective-permute-start
Sparse Core Ops, SparseCore 0:
  9.9 20.8 all-gather.14
  308.0 105.7 all-gather.10
  415.6 20.2 all-gather.16
  437.5 21.1 all-gather.18
  460.4 45.1 all-gather.12
  525.7 117.2 all-reduce.2
